TPU v7x, 256 devices: a whole 4x4x8 slice. The times are simulated.
256 devices in a mesh: expert: 32 (over z, y_lo, core), blk: 8 (over x, y_hi).
Axes of the slice: x: 4, y: 4 (y_hi: 2, y_lo: 2; y = y_hi * 2 + y_lo), z: 8, core: 2. Of those that a mesh axis runs over, the one named last changes fastest.
Arguments:
- tokens: bfloat16 [16384, 7168], P(('expert', 'blk')), may hold values from -6 to 6
- expert_ids: int32 [16384, 8], P(('expert', 'blk')), may hold values from 0 to 255, all different within a row; in each aligned block of 64 rows (0 to 63, 64 to 127, ...) at most 4 rows name the same one
- gate_weights: bfloat16 [16384, 8], P(('expert', 'blk')), may hold values from 0.099609375 to 1
- w_gate: bfloat16 [32, 7168, 2048], P('expert', None, 'blk'), may hold values from -0.0625 to 0.0625
- w_up: bfloat16 [32, 7168, 2048], P('expert', None, 'blk'), may hold values from -0.0625 to 0.0625
- w_down: bfloat16 [32, 2048, 7168], P('expert', None, 'blk'), may hold values from -0.125 to 0.125
Outputs:
- mixed_out: bfloat16 [16384, 7168], P(('expert', 'blk'))
Inputs may be any that keep to these rules, and one draw needn't show every extreme that they name: `expert_ids`: each row names 8 different experts; among the 64 rows of one device no expert is named more than 4 times, a bound that some block reaches.
All inputs are finite; a program needn't handle non-finite values.
Results may differ from a plain program's by a relative error of at most 0.0057.
Values may be sent and summed in bfloat16 or wider, within the bound.
A program may use at most 64 MiB of HBM per device.

v0:
```python
import jax
import jax.numpy as jnp
from jax import lax
from jax.sharding import PartitionSpec as P

CAP = 4


def slot_tables(id_rows, gate_rows, experts, capacity):
    labels = jnp.arange(experts, dtype=jnp.int32)
    matches = id_rows[:, :, None] == labels[None, None, :]
    chosen = jnp.any(matches, axis=1)
    weights = jnp.sum(jnp.where(matches, gate_rows.astype(jnp.float32)[:, :, None], 0.0), axis=1)
    counts = chosen.astype(jnp.int32)
    before = jnp.cumsum(counts, axis=0) - counts
    places = jnp.arange(capacity, dtype=jnp.int32)
    selected = chosen[:, :, None] & (before[:, :, None] == places[None, None, :])
    selector = selected.astype(jnp.bfloat16)
    weighting = jnp.where(selected, weights[:, :, None], 0.0).astype(jnp.bfloat16)
    return (selector, weighting)


def hidden_units(row_block, gate_mat, up_mat):
    gate_part = jnp.dot(row_block, gate_mat, preferred_element_type=jnp.float32)
    up_part = jnp.dot(row_block, up_mat, preferred_element_type=jnp.float32)
    return (jax.nn.silu(gate_part) * up_part).astype(jnp.bfloat16)


def on_device(tokens, expert_ids, gate_weights, w_gate, w_up, w_down):
    gate_mat = w_gate[0]
    up_mat = w_up[0]
    down_mat = w_down[0]
    experts = lax.axis_size("expert")
    blocks = lax.axis_size("blk")
    tok_dev = tokens.shape[0]
    width = tokens.shape[1]
    selector, weighting = slot_tables(expert_ids, gate_weights, experts, CAP)
    outgoing = jnp.einsum(
        "tec,td->ecd", selector, tokens, preferred_element_type=jnp.float32
    ).astype(jnp.bfloat16)
    received = lax.all_to_all(outgoing, "expert", split_axis=0, concat_axis=0, tiled=True)
    mine = received.reshape(experts * CAP, width)
    row_block = lax.all_gather(mine, "blk", axis=0, tiled=True)
    hidden = hidden_units(row_block, gate_mat, up_mat)
    hidden_all = lax.all_gather(hidden, "blk", axis=1, tiled=True)
    slices = jnp.dot(hidden_all, down_mat, preferred_element_type=jnp.float32).astype(jnp.bfloat16)
    slices = slices.reshape(blocks, experts, CAP, -1).transpose(1, 0, 2, 3)
    slices = slices.reshape(experts, blocks * CAP, -1)
    weighting_all = lax.all_gather(
        weighting.reshape(tok_dev, experts * CAP), "blk", axis=0, tiled=True
    ).reshape(blocks, tok_dev, experts, CAP)
    returned = lax.all_to_all(slices, "expert", split_axis=0, concat_axis=0, tiled=True)
    returned = returned.reshape(experts, blocks, CAP, -1)
    partial_out = jnp.einsum(
        "btec,ebcd->btd", weighting_all, returned, preferred_element_type=jnp.float32
    ).astype(jnp.bfloat16)
    partial_out = partial_out.reshape(blocks * tok_dev, -1)
    return lax.all_to_all(partial_out, "blk", split_axis=0, concat_axis=1, tiled=True)


def solution(mesh):
    return jax.shard_map(
        on_device,
        mesh=mesh,
        in_specs=(
            P(("expert", "blk"), None),
            P(("expert", "blk"), None),
            P(("expert", "blk"), None),
            P("expert", None, "blk"),
            P("expert", None, "blk"),
            P("expert", None, "blk"),
        ),
        out_specs=P(("expert", "blk"), None),
        check_vma=False,
    )
```

profile of v0, /device:TPU:8, one launch (start us, length us, event | category | flops | bytes accessed | tf_op | source)
XLA Modules:
  0.0 427.2 jit_solution(4727964634798736242)
XLA Ops:
  6.5 0.8 fusion.17
  7.7 0.6 convolution_convert_fusion
  8.4 1.4 copy.51
  9.8 55.6 %all_to_all.26 = bf16[32,4,7168]{2,1,0:T(4,128)(2,1)S(1)} all-to-all(bf16[32,4,7168]{2,1,0:T(4,128)(2,1)S(1)} %copy.51), channel_id=1, replica_groups=mesh['expert'=32,'blk'=8] {'expert'}, dimensions={0} | all-to-all | bytes 3670016 | tf_op jit(solution)/shard_map/all_to_all | solution.py:41
  65.4 1.4 reshape.42
  66.9 0.2 all-gather.5.cloned.1.call-start
  67.1 166.8 %all-gather.3.cloned.1.call-done = bf16[1024,7168]{1,0:T(8,128)(2,1)} async-done(((bf16[128,7168]{1,0:T(8,128)(2,1)}), bf16[1024,7168]{1,0:T(8,128)(2,1)}) %all-gather.3.cloned.1.call-update) | async-done | bytes 14680080 | tf_op jit(solution)/shard_map/all_gather | solution.py:43
  233.9 8.8 %fusion.4 = f32[1024,256]{1,0:T(8,128)S(1)} fusion(bf16[1024,7168]{1,0:T(8,128)(2,1)} %all-gather.3.cloned.1.call-done, bf16[1,7168,256]{2,1,0:T(8,128)(2,1)} %param.9), kind=kOutput, calls=%fused_computation.5 | convolution fusion | flops 3758096384 | bytes 19398656 | tf_op jit(solution)/shard_map/dot_general | solution.py:24
  242.7 1.5 copy-done.3
  244.3 1.0 copy-done.4
  245.3 4.8 %fusion.12 = bf16[1024,256]{1,0:T(8,128)(2,1)} fusion(bf16[1024,7168]{1,0:T(8,128)(2,1)S(1)} %copy-done.3, bf16[1,7168,256]{2,1,0:T(8,128)(2,1)S(1)} %copy-done.4, f32[1024,256]{1,0:T(8,128)S(1)} %fusion.4), kind=kOutput, calls=%fused_computation.10 | convolution fusion | flops 3759669248 | bytes 19922944 | tf_op jit(solution)/shard_map/dot_general | solution.py:25
  250.1 80.3 %all-gather.5.cloned.1.call-done = bf16[1024,2048]{1,0:T(8,128)(2,1)} async-done(((bf16[1024,256]{1,0:T(8,128)(2,1)}), bf16[1024,2048]{1,0:T(8,128)(2,1)}) %all-gather.5.cloned.1.call-update) | async-done | bytes 4194320 | tf_op jit(solution)/shard_map/all_gather | solution.py:45
  330.4 9.1 %fusion.6 = bf16[1024,896]{1,0:T(8,128)(2,1)} fusion(bf16[1024,2048]{1,0:T(8,128)(2,1)} %all-gather.5.cloned.1.call-done, bf16[1,2048,896]{2,1,0:T(8,128)(2,1)} %param.11), kind=kOutput, calls=%fused_computation.8 | convolution fusion | flops 3759013888 | bytes 9699328 | tf_op jit(solution)/shard_map/dot_general | solution.py:46
  339.5 3.1 reshape.43
  342.6 0.3 copy.52
  342.9 1.8 copy.53
  344.8 8.6 %all-to-all-start.1 = ((bf16[32,32,896]{2,1,0:T(8,128)(2,1)}), bf16[32,32,896]{2,1,0:T(8,128)(2,1)S(1)}, u32[]{:S(2)}, u32[]{:S(2)}) async-start(bf16[32,32,896]{2,1,0:T(8,128)(2,1)} %copy.53), calls=%async_computation.1 | async-start | bytes 3670016 | tf_op jit(solution)/shard_map/all_to_all | solution.py:52
  353.9 34.7 %all_gather.9 = bf16[512,128]{1,0:T(8,128)(2,1)S(1)} all-gather(bf16[64,128]{1,0:T(8,128)(2,1)S(1)} %select_convert_fusion), channel_id=1, replica_groups=mesh['expert'=32,'blk'=8] {'blk'}, dimensions={0}, use_global_device_ids=true | all-gather | bytes 147456 | tf_op jit(solution)/shard_map/all_gather | solution.py:49
  388.7 0.2 reshape.41
  388.9 9.2 %all-to-all-done.1 = bf16[32,32,896]{2,1,0:T(8,128)(2,1)S(1)} async-done(((bf16[32,32,896]{2,1,0:T(8,128)(2,1)}), bf16[32,32,896]{2,1,0:T(8,128)(2,1)S(1)}, u32[]{:S(2)}, u32[]{:S(2)}) %all-to-all-start.1) | async-done | bytes 1835040 | tf_op jit(solution)/shard_map/all_to_all | solution.py:52
  398.1 0.6 copy.54
  398.6 0.5 bitcast_convert_fusion
  399.1 20.2 %all_to_all.27 = bf16[8,64,896]{2,1,0:T(8,128)(2,1)S(1)} all-to-all(bf16[8,64,896]{2,1,0:T(8,128)(2,1)S(1)} %bitcast_convert_fusion), channel_id=1, replica_groups=mesh['expert'=32,'blk'=8] {'blk'}, dimensions={0} | all-to-all | bytes 1835008 | tf_op jit(solution)/shard_map/all_to_all | solution.py:58
  419.3 1.1 copy.58
  (29 shorter events, 1.0 us)
Async XLA Ops:
  6.5 1.2 copy-start
  6.5 227.3 %all-gather.3.cloned.1.call-start = ((), (), s32[]{:S(2)}) async-start(), calls=%async_computation.3 | async-start | bytes 16515072 | tf_op jit(solution)/shard_map/all_gather | solution.py:43
  66.9 263.5 %all-gather.5.cloned.1.call-start = ((), (), s32[]{:S(2)}) async-start(), calls=%async_computation.4 | async-start | bytes 4718592 | tf_op jit(solution)/shard_map/all_gather | solution.py:45
  233.9 10.4 %copy-start.3 = (bf16[1024,7168]{1,0:T(8,128)(2,1)S(1)}, bf16[1024,7168]{1,0:T(8,128)(2,1)}, u32[]{:S(2)}) copy-start(bf16[1024,7168]{1,0:T(8,128)(2,1)} %all-gather.3.cloned.1.call-done) | copy-start | bytes 44040196
  233.9 11.4 %copy-start.4 = (bf16[1,7168,256]{2,1,0:T(8,128)(2,1)S(1)}, bf16[1,7168,256]{2,1,0:T(8,128)(2,1)}, u32[]{:S(2)}) copy-start(bf16[1,7168,256]{2,1,0:T(8,128)(2,1)} %param.10) | copy-start | bytes 11010052
  342.9 10.7 %copy-start.2 = (bf16[64,8]{0,1:T(8,128)(2,1)S(1)}, bf16[64,8]{0,1:T(8,128)(2,1)}, u32[]{:S(2)}) copy-start(bf16[64,8]{0,1:T(8,128)(2,1)} %param.8) | copy-start | bytes 3076
  342.9 10.7 %copy-start.1 = (s32[64,8]{0,1:T(8,128)S(1)}, s32[64,8]{0,1:T(8,128)}, u32[]{:S(2)}) copy-start(s32[64,8]{0,1:T(8,128)} %param.7) | copy-start | bytes 6148
  344.8 53.3 %all-to-all-start.1 = ((bf16[32,32,896]{2,1,0:T(8,128)(2,1)}), bf16[32,32,896]{2,1,0:T(8,128)(2,1)S(1)}, u32[]{:S(2)}, u32[]{:S(2)}) async-start(bf16[32,32,896]{2,1,0:T(8,128)(2,1)} %copy.53), calls=%async_computation.1 | async-start | bytes 3670016 | tf_op jit(solution)/shard_map/all_to_all | solution.py:52
Sparse Core Ops, SparseCore 0:
  67.0 166.8 all-gather.2
  250.2 80.1 all-gather.4
where the time goes:
time: 427 us
  waiting for transfers between devices  256 us (60%)
  blocking collectives  110 us (26%)
  matrix products  23.8 us (6%)
  between operations  13.6 us (3%)
  local copies, waits for them, and re-layouts  13.3 us (3%)
  starting transfers between devices  8.85 us (2%)
    all_gather x1, waiting for transfers between devices, on_device(): row_block = lax.all_gather(mine, 'blk', axis=0, tiled=True)  167 us
    all_gather x1, waiting for transfers between devices, on_device(): hidden_all = lax.all_gather(hidden, 'blk', axis=1, tiled=True)  80.3 us
    all_to_all x1, blocking collectives, on_device(): lax.all_to_all(outgoing, 'expert', split_axis=0, concat_axis=0, tiled=True)  55.6 us
    all_gather x1, blocking collectives, on_device(): lax.all_gather(weighting.reshape(tok_dev, experts * CAP), 'blk', axis=0,...  34.7 us
    all_to_all x1, blocking collectives, on_device(): lax.all_to_all(partial_out, 'blk', split_axis=0, concat_axis=1, tiled=True)  20.2 us
    all_to_all x1, waiting for transfers between devices, on_device(): lax.all_to_all(slices, 'expert', split_axis=0, concat_axis=0, tiled=True)  9.15 us
    dot_general x1, matrix products, on_device(): jnp.dot(hidden_all, down_mat, preferred_element_type=jnp.float32)  9.07 us
    dot_general x1, matrix products, hidden_units(): gate_part = jnp.dot(row_block, gate_mat, preferred_element_type=jnp.float32)  8.83 us
  transfers between devices with their start and end apart: 3, of which 3 were waited for; matrix products, arithmetic and copies ran while one was open for 0% of the time, Pallas kernels for 0%

commit v1 on v0

--- a/solution.py
+++ b/solution.py
@@ -40,7 +40,10 @@
     ).astype(jnp.bfloat16)
     received = lax.all_to_all(outgoing, "expert", split_axis=0, concat_axis=0, tiled=True)
     mine = received.reshape(experts * CAP, width)
-    row_block = lax.all_gather(mine, "blk", axis=0, tiled=True)
+    peers = lax.axis_size("blk")
+    pieces = jnp.stack([mine for _ in range(peers)])
+    pieces = lax.all_to_all(pieces, "blk", split_axis=0, concat_axis=0)
+    row_block = jnp.concatenate(pieces, axis=0)
     hidden = hidden_units(row_block, gate_mat, up_mat)
     hidden_all = lax.all_gather(hidden, "blk", axis=1, tiled=True)
     slices = jnp.dot(hidden_all, down_mat, preferred_element_type=jnp.float32).astype(jnp.bfloat16)

time: 427 us -> 423 us (level)
  blocking collectives: 110 us -> 279 us
  waiting for transfers between devices: 256 us -> 87.2 us
  matrix products: 23.8 us -> 18.9 us
    all_to_all x0 -> x1, blocking collectives: none -> 169 us  [on_device(): pieces = lax.all_to_all(pieces, 'blk', split_axis=0, concat_axis=0)]
    all_gather x1 -> x0, waiting for transfers between devices: 167 us -> none  [on_device(): row_block = lax.all_gather(mine, 'blk', axis=0, tiled=True)]
    another operation x0 -> x2, local copies, waits for them, and re-layouts: none -> 5.18 us  [on_device(): pieces = jnp.stack([mine for _ in range(peers)])]
    dot_general x1, matrix products: 8.83 us -> 3.94 us  [hidden_units(): gate_part = jnp.dot(row_block, gate_mat, preferred_element_type=jnp.float32)]
  transfers between devices with their start and end apart: 3 -> 2, of which waited for: 3 -> 2; matrix products, arithmetic and copies ran while one was open for 0% -> 0% of each run, Pallas kernels for 0% -> 0%
where the time goes in v1:
time: 423 us
  blocking collectives  279 us (66%)
  waiting for transfers between devices  87.2 us (21%)
  matrix products  18.9 us (4%)
  local copies, waits for them, and re-layouts  14.4 us (3%)
  between operations  13.6 us (3%)
  starting transfers between devices  8.63 us (2%)
    all_to_all x1, blocking collectives, on_device(): pieces = lax.all_to_all(pieces, 'blk', split_axis=0, concat_axis=0)  169 us
    all_gather x1, waiting for transfers between devices, on_device(): hidden_all = lax.all_gather(hidden, 'blk', axis=1, tiled=True)  78 us
    all_to_all x1, blocking collectives, on_device(): lax.all_to_all(outgoing, 'expert', split_axis=0, concat_axis=0, tiled=True)  55.6 us
    all_gather x1, blocking collectives, on_device(): lax.all_gather(weighting.reshape(tok_dev, experts * CAP), 'blk', axis=0,...  34.7 us
    all_to_all x1, blocking collectives, on_device(): lax.all_to_all(partial_out, 'blk', split_axis=0, concat_axis=1, tiled=True)  20.2 us
    all_to_all x1, waiting for transfers between devices, on_device(): lax.all_to_all(slices, 'expert', split_axis=0, concat_axis=0, tiled=True)  9.16 us
    dot_general x1, matrix products, on_device(): jnp.dot(hidden_all, down_mat, preferred_element_type=jnp.float32)  9.07 us
    all_to_all x1, starting transfers between devices, on_device(): lax.all_to_all(slices, 'expert', split_axis=0, concat_axis=0, tiled=True)  8.62 us
  transfers between devices with their start and end apart: 2, of which 2 were waited for; matrix products, arithmetic and copies ran while one was open for 0% of the time, Pallas kernels for 0%

profile of v1, /device:TPU:8, one launch (start us, length us, event | category | flops | bytes accessed | tf_op | source)
XLA Modules:
  0.0 423.0 jit_solution(14849046578476247793)
XLA Ops:
  6.5 0.8 fusion.17
  7.7 0.6 convolution_convert_fusion
  8.4 1.4 copy.51
  9.8 55.6 %all_to_all.31 = bf16[32,4,7168]{2,1,0:T(4,128)(2,1)S(1)} all-to-all(bf16[32,4,7168]{2,1,0:T(4,128)(2,1)S(1)} %copy.51), channel_id=1, replica_groups=mesh['expert'=32,'blk'=8] {'expert'}, dimensions={0} | all-to-all | bytes 3670016 | tf_op jit(solution)/shard_map/all_to_all | solution.py:41
  65.4 1.5 stack_reshape.2
  66.9 3.7 stack.3
  70.6 168.8 %all_to_all.32 = bf16[8,128,7168]{2,1,0:T(8,128)(2,1)S(1)} all-to-all(bf16[8,128,7168]{2,1,0:T(8,128)(2,1)S(1)} %stack.3), channel_id=1, replica_groups=mesh['expert'=32,'blk'=8] {'blk'}, dimensions={0} | all-to-all | bytes 29360128 | tf_op jit(solution)/shard_map/all_to_all | solution.py:45
  239.5 3.9 fusion.4
  243.4 4.8 %fusion.12 = bf16[1024,256]{1,0:T(8,128)(2,1)} fusion(bf16[1024,7168]{1,0:T(8,128)(2,1)S(1)} %bitcast.39, bf16[1,7168,256]{2,1,0:T(8,128)(2,1)S(1)} %copy-done.5, f32[1024,256]{1,0:T(8,128)S(1)} %fusion.4), kind=kOutput, calls=%fused_computation.10 | convolution fusion | flops 3759669248 | bytes 19922944 | tf_op jit(solution)/shard_map/dot_general | solution.py:25
  248.2 78.0 %all-gather.2.cloned.1.call-done = bf16[1024,2048]{1,0:T(8,128)(2,1)} async-done(((bf16[1024,256]{1,0:T(8,128)(2,1)}), bf16[1024,2048]{1,0:T(8,128)(2,1)}) %all-gather.2.cloned.1.call-update) | async-done | bytes 4194320 | tf_op jit(solution)/shard_map/all_gather | solution.py:48
  326.2 9.1 %fusion.6 = bf16[1024,896]{1,0:T(8,128)(2,1)} fusion(bf16[1024,2048]{1,0:T(8,128)(2,1)} %all-gather.2.cloned.1.call-done, bf16[1,2048,896]{2,1,0:T(8,128)(2,1)} %param.11), kind=kOutput, calls=%fused_computation.8 | convolution fusion | flops 3759013888 | bytes 9699328 | tf_op jit(solution)/shard_map/dot_general | solution.py:49
  335.3 3.1 reshape.45
  338.4 0.3 copy.52
  338.7 1.8 copy.53
  340.6 8.6 %all-to-all-start.2 = ((bf16[32,32,896]{2,1,0:T(8,128)(2,1)}), bf16[32,32,896]{2,1,0:T(8,128)(2,1)S(1)}, u32[]{:S(2)}, u32[]{:S(2)}) async-start(bf16[32,32,896]{2,1,0:T(8,128)(2,1)} %copy.53), calls=%async_computation.2 | async-start | bytes 3670016 | tf_op jit(solution)/shard_map/all_to_all | solution.py:55
  349.6 0.1 eq.43
  349.7 34.7 %all_gather.6 = bf16[512,128]{1,0:T(8,128)(2,1)S(1)} all-gather(bf16[64,128]{1,0:T(8,128)(2,1)S(1)} %select_convert_fusion), channel_id=1, replica_groups=mesh['expert'=32,'blk'=8] {'blk'}, dimensions={0}, use_global_device_ids=true | all-gather | bytes 147456 | tf_op jit(solution)/shard_map/all_gather | solution.py:52
  384.4 0.1 copy.49
  384.5 0.2 reshape.43
  384.7 9.2 %all-to-all-done.2 = bf16[32,32,896]{2,1,0:T(8,128)(2,1)S(1)} async-done(((bf16[32,32,896]{2,1,0:T(8,128)(2,1)}), bf16[32,32,896]{2,1,0:T(8,128)(2,1)S(1)}, u32[]{:S(2)}, u32[]{:S(2)}) %all-to-all-start.2) | async-done | bytes 1835040 | tf_op jit(solution)/shard_map/all_to_all | solution.py:55
  393.9 0.6 copy.54
  394.4 0.5 bitcast_convert_fusion
  394.9 20.2 %all_to_all.33 = bf16[8,64,896]{2,1,0:T(8,128)(2,1)S(1)} all-to-all(bf16[8,64,896]{2,1,0:T(8,128)(2,1)S(1)} %bitcast_convert_fusion), channel_id=1, replica_groups=mesh['expert'=32,'blk'=8] {'blk'}, dimensions={0} | all-to-all | bytes 1835008 | tf_op jit(solution)/shard_map/all_to_all | solution.py:61
  415.1 1.1 copy.58
  (30 shorter events, 0.8 us)
Async XLA Ops:
  6.5 1.2 copy-start
  6.5 319.7 %all-gather.2.cloned.1.call-start = ((), (), s32[]{:S(2)}) async-start(), calls=%async_computation.4 | async-start | bytes 4718592 | tf_op jit(solution)/shard_map/all_gather | solution.py:48
  70.6 168.8 %copy-start.4 = (bf16[1,7168,256]{2,1,0:T(8,128)(2,1)S(1)}, bf16[1,7168,256]{2,1,0:T(8,128)(2,1)}, u32[]{:S(2)}) copy-start(bf16[1,7168,256]{2,1,0:T(8,128)(2,1)} %param.9) | copy-start | bytes 11010052
  239.5 4.0 copy-start.5
  338.7 10.7 %copy-start.3 = (bf16[64,8]{0,1:T(8,128)(2,1)S(1)}, bf16[64,8]{0,1:T(8,128)(2,1)}, u32[]{:S(2)}) copy-start(bf16[64,8]{0,1:T(8,128)(2,1)} %param.8) | copy-start | bytes 3076
  338.7 10.7 %copy-start.2 = (s32[64,8]{0,1:T(8,128)S(1)}, s32[64,8]{0,1:T(8,128)}, u32[]{:S(2)}) copy-start(s32[64,8]{0,1:T(8,128)} %param.7) | copy-start | bytes 6148
  340.6 53.3 %all-to-all-start.2 = ((bf16[32,32,896]{2,1,0:T(8,128)(2,1)}), bf16[32,32,896]{2,1,0:T(8,128)(2,1)S(1)}, u32[]{:S(2)}, u32[]{:S(2)}) async-start(bf16[32,32,896]{2,1,0:T(8,128)(2,1)} %copy.53), calls=%async_computation.2 | async-start | bytes 3670016 | tf_op jit(solution)/shard_map/all_to_all | solution.py:55
  393.9 22.3 %copy-start.1 = (bf16[64,7168]{1,0:T(8,128)(2,1)S(1)}, bf16[64,7168]{1,0:T(8,128)(2,1)}, u32[]{:S(2)}) copy-start(bf16[64,7168]{1,0:T(8,128)(2,1)} %param.6) | copy-start | bytes 2752516
Sparse Core Ops, SparseCore 0:
  248.3 77.8 all-gather.1
